TPU v7x, 32 devices: a whole 2x2x4 slice. The times are simulated.
32 devices in a mesh: dp: 4 (over x, core), group: 4 (over z), tensor: 2 (over y).
Axes of the slice: x: 2, y: 2, z: 4, core: 2. Of those that a mesh axis runs over, the one named last changes fastest.
Arguments:
- residual_in: bfloat16 [32, 1024, 767], P(('dp', 'group'), 'tensor'), may hold values from -6 to 6
- piece_ids: int32 [32, 1024], P(('dp', 'group')), may hold values from -1 to 3, as said below
- norm_gains: bfloat16 [2, 768], replicated, may hold values from 0.25 to 1.75
- qkv_weight: bfloat16 [3, 768, 768], P(None, None, 'tensor'), may hold values from -0.21875 to 0.21875
- qv_bias: bfloat16 [2, 768], P(None, 'tensor'), may hold values from -3 to 3
- out_weight: bfloat16 [768, 767], P('tensor'), may hold values from -0.875 to 0.875
- fc_weight: bfloat16 [768, 3072], P(None, 'tensor'), may hold values from -0.21875 to 0.21875
- fc_bias: bfloat16 [3072], P('tensor'), may hold values from -3 to 3
- proj_weight: bfloat16 [3072, 767], P('tensor'), may hold values from -0.109375 to 0.109375
- out_biases: bfloat16 [2, 767], replicated, may hold values from -2 to 2
- cotangent: bfloat16 [32, 1024, 767], P(('dp', 'group'), 'tensor'), may hold values from -6 to 6
Outputs:
- block_out: bfloat16 [32, 1024, 767], P(('dp', 'group'), 'tensor')
- grad_input: bfloat16 [32, 1024, 767], P(('dp', 'group'), 'tensor')
- grad_gains: float32 [2, 768], replicated
- grad_qkv: float32 [3, 768, 768], P(None, 'dp', 'tensor')
- grad_qv_bias: float32 [2, 768], P(None, ('tensor', 'dp'))
- grad_out_weight: float32 [768, 767], P(('tensor', 'dp'))
- grad_fc_weight: float32 [768, 3072], P('dp', 'tensor')
- grad_fc_bias: float32 [3072], P(('tensor', 'dp'))
- grad_proj_weight: float32 [3072, 767], P(('tensor', 'dp'))
- grad_out_biases: float32 [2, 767], replicated
Inputs may be any that keep to these rules, and one draw needn't show every extreme that they name: `piece_ids`: each aligned block of 256 positions of a sequence carries one id: -1 (text) or the block's own number (a picture piece). The first block of every sequence is text and the last one a picture piece.
All inputs are finite; a program needn't handle non-finite values.
Results may differ from a plain program's by a relative error of at most 0.02.
Values may be sent and summed in bfloat16 or wider, within the bound.
No kernel may reach another device: no remote copies, remote signals or barrier semaphores. Data moves between devices by JAX's collectives and lax.ppermute only.
A program may use at most 192 MiB of HBM per device.

v0:
```python
import jax
import jax.numpy as jnp
from jax import lax
from jax.sharding import PartitionSpec as P

D = 768
HD = 64
EPSILON = 1e-05
MASKED = -1e30


def decompress(compact):
    return jnp.concatenate([compact, -jnp.sum(compact, axis=-1, keepdims=True)], axis=-1)


def crms_gain(compact, gain):
    full_rows = decompress(compact)
    factor = lax.rsqrt(jnp.mean(full_rows * full_rows, axis=-1, keepdims=True) + EPSILON)
    return full_rows * factor * gain


def gelu_tanh(values):
    return jax.nn.gelu(values, approximate=True)


def visible_mask(labels, row_start, row_count):
    query_pos = row_start + jnp.arange(row_count)
    key_pos = jnp.arange(labels.shape[0])
    row_labels = labels[row_start : row_start + row_count]
    causal = key_pos[None, :] <= query_pos[:, None]
    inside = (row_labels[:, None] == labels[None, :]) & (row_labels[:, None] >= 0)
    return causal | inside


def block_scores(row_query, key_rows, labels, row_start, row_block):
    scores = jnp.einsum(
        "qhd,khd->hqk", row_query, key_rows, preferred_element_type=jnp.float32
    ) * HD ** (-0.5)
    return jnp.where(visible_mask(labels, row_start, row_block)[None], scores, MASKED)


def attend_forward(inputs):
    queries, key_rows, value_rows, labels = inputs
    length = key_rows.shape[0]
    row_block = min(512, length)
    outputs = []
    log_parts = []
    for row_start in range(0, length, row_block):
        scores = block_scores(
            queries[row_start : row_start + row_block], key_rows, labels, row_start, row_block
        )
        highest = jnp.max(scores, axis=-1, keepdims=True)
        weights = jnp.exp(scores - highest)
        weight_sum = jnp.sum(weights, axis=-1, keepdims=True)
        prob_low = (weights / weight_sum).astype(jnp.bfloat16)
        outputs.append(
            jnp.einsum(
                "hqk,khd->qhd", prob_low, value_rows, preferred_element_type=jnp.float32
            ).astype(jnp.bfloat16)
        )
        log_parts.append((highest + jnp.log(weight_sum))[..., 0])
    return (jnp.concatenate(outputs, 0), jnp.concatenate(log_parts, 1))


def attend_backward(inputs):
    queries, key_rows, value_rows, labels, upstream, log_sums = inputs
    length = key_rows.shape[0]
    row_block = min(512, length)
    score_scale = HD ** (-0.5)
    grad_keys = jnp.zeros(key_rows.shape, jnp.float32)
    grad_values = jnp.zeros(value_rows.shape, jnp.float32)
    query_grads = []
    for row_start in range(0, length, row_block):
        row_query = queries[row_start : row_start + row_block]
        row_up = upstream[row_start : row_start + row_block]
        scores = block_scores(row_query, key_rows, labels, row_start, row_block)
        probs = jnp.exp(scores - log_sums[:, row_start : row_start + row_block, None])
        along = jnp.einsum("qhd,khd->hqk", row_up, value_rows, preferred_element_type=jnp.float32)
        inner = jnp.sum(along * probs, axis=-1, keepdims=True)
        score_grad = (probs * (along - inner)).astype(jnp.bfloat16)
        query_grads.append(
            jnp.einsum("hqk,khd->qhd", score_grad, key_rows, preferred_element_type=jnp.float32)
            * score_scale
        )
        grad_keys = (
            grad_keys
            + jnp.einsum("hqk,qhd->khd", score_grad, row_query, preferred_element_type=jnp.float32)
            * score_scale
        )
        grad_values = grad_values + jnp.einsum(
            "hqk,qhd->khd", probs.astype(jnp.bfloat16), row_up, preferred_element_type=jnp.float32
        )
    return (jnp.concatenate(query_grads, 0), grad_keys, grad_values)


def on_device(
    residual_in,
    piece_ids,
    norm_gains,
    qkv_weight,
    qv_bias,
    out_weight,
    fc_weight,
    fc_bias,
    proj_weight,
    out_biases,
    cotangent,
):
    residual_rows, upstream_rows, labels_all = (residual_in, cotangent, piece_ids)
    qkv_w, qv_b, out_w, fc_w, fc_b, proj_w = (
        qkv_weight,
        qv_bias,
        out_weight,
        fc_weight,
        fc_bias,
        proj_weight,
    )
    seq_count, local_len, compact_width = residual_rows.shape
    local_rows = seq_count * local_len
    local_width = qkv_w.shape[2]
    head_count = local_width // HD
    gain_values = norm_gains.astype(jnp.float32)
    bias_values = qv_b.astype(jnp.float32)
    end_biases = out_biases.astype(jnp.float32)
    inputs_flat = residual_rows.reshape(local_rows, compact_width).astype(jnp.float32)
    normed_one, norm_one_back = jax.vjp(crms_gain, inputs_flat, gain_values[0])
    one_low = normed_one.astype(jnp.bfloat16).reshape(seq_count, local_len, D)
    full_one = lax.all_gather(one_low, "tensor", axis=1, tiled=True)
    seq_len = full_one.shape[1]
    token_count = seq_count * seq_len
    flat_one = full_one.reshape(token_count, D)
    projected = jnp.einsum("td,cde->cte", flat_one, qkv_w, preferred_element_type=jnp.float32)
    queries = (
        (projected[0] + bias_values[0])
        .astype(jnp.bfloat16)
        .reshape(seq_count, seq_len, head_count, HD)
    )
    key_rows = projected[1].astype(jnp.bfloat16).reshape(seq_count, seq_len, head_count, HD)
    value_rows = (
        (projected[2] + bias_values[1])
        .astype(jnp.bfloat16)
        .reshape(seq_count, seq_len, head_count, HD)
    )
    attended, log_sums = lax.map(attend_forward, (queries, key_rows, value_rows, labels_all))
    attended_flat = attended.reshape(token_count, local_width)
    branch_part = jnp.dot(attended_flat, out_w, preferred_element_type=jnp.float32).reshape(
        seq_count, seq_len, compact_width
    )
    branch_sum = lax.psum_scatter(
        branch_part.astype(jnp.bfloat16), "tensor", scatter_dimension=1, tiled=True
    ).astype(jnp.float32)
    middle = inputs_flat + branch_sum.reshape(local_rows, compact_width) + end_biases[0]
    normed_two, norm_two_back = jax.vjp(crms_gain, middle, gain_values[1])
    two_low = normed_two.astype(jnp.bfloat16).reshape(seq_count, local_len, D)
    full_two = lax.all_gather(two_low, "tensor", axis=1, tiled=True).reshape(token_count, D)
    hidden_pre = jnp.dot(full_two, fc_w, preferred_element_type=jnp.float32) + fc_b.astype(
        jnp.float32
    )
    active_full, gelu_back = jax.vjp(gelu_tanh, hidden_pre)
    active = active_full.astype(jnp.bfloat16)
    mlp_part = jnp.dot(active, proj_w, preferred_element_type=jnp.float32).reshape(
        seq_count, seq_len, compact_width
    )
    mlp_sum = lax.psum_scatter(
        mlp_part.astype(jnp.bfloat16), "tensor", scatter_dimension=1, tiled=True
    ).astype(jnp.float32)
    block_out = (
        (middle + mlp_sum.reshape(local_rows, compact_width) + end_biases[1])
        .astype(jnp.bfloat16)
        .reshape(seq_count, local_len, compact_width)
    )
    upstream_full = lax.all_gather(upstream_rows, "tensor", axis=1, tiled=True).reshape(
        token_count, compact_width
    )
    upstream_flat = upstream_rows.reshape(local_rows, compact_width).astype(jnp.float32)
    grad_proj_weight = jnp.dot(active.T, upstream_full, preferred_element_type=jnp.float32)
    hidden_grad = gelu_back(jnp.dot(upstream_full, proj_w.T, preferred_element_type=jnp.float32))[
        0
    ].astype(jnp.bfloat16)
    grad_fc_weight = jnp.dot(full_two.T, hidden_grad, preferred_element_type=jnp.float32)
    grad_fc_bias = jnp.sum(hidden_grad.astype(jnp.float32), axis=0)
    two_part = jnp.dot(hidden_grad, fc_w.T, preferred_element_type=jnp.float32).reshape(
        seq_count, seq_len, D
    )
    two_grad = (
        lax.psum_scatter(two_part.astype(jnp.bfloat16), "tensor", scatter_dimension=1, tiled=True)
        .astype(jnp.float32)
        .reshape(local_rows, D)
    )
    middle_norm_grad, gain_two_grad = norm_two_back(two_grad)
    middle_grad = upstream_flat + middle_norm_grad
    branch_low = middle_grad.astype(jnp.bfloat16)
    branch_seq = branch_low.reshape(seq_count, local_len, compact_width)
    branch_full = lax.all_gather(branch_seq, "tensor", axis=1, tiled=True).reshape(
        token_count, compact_width
    )
    grad_out_weight = jnp.dot(attended_flat.T, branch_full, preferred_element_type=jnp.float32)
    attended_grad = (
        jnp.dot(branch_full, out_w.T, preferred_element_type=jnp.float32)
        .astype(jnp.bfloat16)
        .reshape(seq_count, seq_len, head_count, HD)
    )
    query_grad, key_grad, value_grad = lax.map(
        attend_backward, (queries, key_rows, value_rows, labels_all, attended_grad, log_sums)
    )
    stacked = (
        jnp.stack([query_grad, key_grad, value_grad])
        .astype(jnp.bfloat16)
        .reshape(3, token_count, local_width)
    )
    grad_qkv = jnp.einsum("td,cte->cde", flat_one, stacked, preferred_element_type=jnp.float32)
    grad_qv_bias = jnp.stack(
        [
            jnp.sum(stacked[0].astype(jnp.float32), axis=0),
            jnp.sum(stacked[2].astype(jnp.float32), axis=0),
        ]
    )
    one_part = jnp.einsum(
        "cte,cde->td", stacked, qkv_w, preferred_element_type=jnp.float32
    ).reshape(seq_count, seq_len, D)
    one_grad = (
        lax.psum_scatter(one_part.astype(jnp.bfloat16), "tensor", scatter_dimension=1, tiled=True)
        .astype(jnp.float32)
        .reshape(local_rows, D)
    )
    input_norm_grad, gain_one_grad = norm_one_back(one_grad)
    grad_input = (
        (middle_grad + input_norm_grad)
        .astype(jnp.bfloat16)
        .reshape(seq_count, local_len, compact_width)
    )
    gain_terms = jnp.stack([gain_one_grad, gain_two_grad])
    bias_terms = jnp.stack(
        [jnp.sum(branch_low.astype(jnp.float32), axis=0), jnp.sum(upstream_flat, axis=0)]
    )
    grad_gains, grad_out_biases = lax.psum((gain_terms, bias_terms), ("dp", "group", "tensor"))
    weight_grads = (
        grad_qkv,
        grad_qv_bias,
        grad_out_weight,
        grad_fc_weight,
        grad_fc_bias,
        grad_proj_weight,
    )
    shards = (
        lax.psum_scatter(
            weight_grads[0].astype(jnp.bfloat16), "dp", scatter_dimension=1, tiled=True
        ).astype(jnp.float32),
        lax.psum_scatter(
            weight_grads[1].astype(jnp.bfloat16), "dp", scatter_dimension=1, tiled=True
        ).astype(jnp.float32),
        lax.psum_scatter(
            weight_grads[2].astype(jnp.bfloat16), "dp", scatter_dimension=0, tiled=True
        ).astype(jnp.float32),
        lax.psum_scatter(
            weight_grads[3].astype(jnp.bfloat16), "dp", scatter_dimension=0, tiled=True
        ).astype(jnp.float32),
        lax.psum_scatter(
            weight_grads[4].astype(jnp.bfloat16), "dp", scatter_dimension=0, tiled=True
        ).astype(jnp.float32),
        lax.psum_scatter(
            weight_grads[5].astype(jnp.bfloat16), "dp", scatter_dimension=0, tiled=True
        ).astype(jnp.float32),
    )
    reduced = (
        lax.psum(shards[0].astype(jnp.bfloat16), "group").astype(jnp.float32),
        lax.psum(shards[1].astype(jnp.bfloat16), "group").astype(jnp.float32),
        lax.psum(shards[2].astype(jnp.bfloat16), "group").astype(jnp.float32),
        lax.psum(shards[3].astype(jnp.bfloat16), "group").astype(jnp.float32),
        lax.psum(shards[4].astype(jnp.bfloat16), "group").astype(jnp.float32),
        lax.psum(shards[5].astype(jnp.bfloat16), "group").astype(jnp.float32),
    )
    return (
        block_out,
        grad_input,
        grad_gains,
        reduced[0],
        reduced[1],
        reduced[2],
        reduced[3],
        reduced[4],
        reduced[5],
        grad_out_biases,
    )


def solution(mesh):
    in_specs = (
        P(("dp", "group"), "tensor", None),
        P(("dp", "group"), None),
        P(),
        P(None, None, "tensor"),
        P(None, "tensor"),
        P("tensor", None),
        P(None, "tensor"),
        P("tensor"),
        P("tensor", None),
        P(),
        P(("dp", "group"), "tensor", None),
    )
    out_specs = (
        P(("dp", "group"), "tensor", None),
        P(("dp", "group"), "tensor", None),
        P(),
        P(None, "dp", "tensor"),
        P(None, ("tensor", "dp")),
        P(("tensor", "dp"), None),
        P("dp", "tensor"),
        P(("tensor", "dp")),
        P(("tensor", "dp"), None),
        P(),
    )
    return jax.shard_map(
        on_device, mesh=mesh, in_specs=in_specs, out_specs=out_specs, check_vma=False
    )
```

profile of v0, /device:TPU:0, one launch (start us, length us, event | category | flops | bytes accessed | tf_op | source)
XLA Modules:
  0.0 1026.2 jit_solution(11230917446306738538)
XLA Ops:
  28.7 47.5 %all-gather.5.cloned.1.call-done = bf16[2,1024,768]{2,1,0:T(8,128)(2,1)} async-done(((bf16[2,512,768]{2,1,0:T(8,128)(2,1)}), bf16[2,1024,768]{2,1,0:T(8,128)(2,1)}) %all-gather.5.cloned.1.call-update) | async-done | bytes 3145744 | tf_op jit(solution)/shard_map/all_gather | solution.py:128
  124.6 54.4 %while.26 = (s32[]{:T(128)}, bf16[2,1024,6,64]{1,3,2,0:T(8,128)(2,1)}, f32[2,6,1024]{2,1,0:T(8,128)}, bf16[2,1024,6,64]{1,3,2,0:T(8,128)(2,1)}, s32[2,1024]{1,0:...) while((s32[]{:T(128)}, ...), condition=%wide.region_7.8_spmd, body=%wide.region_2.7_spmd.sunk | while | flops 1692272128 | bytes 111457016 | solution.py:144
  185.3 42.1 %reduce-scatter.14.cloned.1.call-done = bf16[2,512,767]{2,1,0:T(8,128)(2,1)} async-done(((bf16[2,1024,767]{2,1,0:T(8,128)(2,1)}), bf16[2,512,767]{2,1,0:T(8,128)(2,1)}) %reduce-scatter.14.cloned.1.call-update) | async-done | bytes 1570832 | tf_op jit(solution)/shard_map/reduce_scatter | solution.py:149
  244.4 29.4 %all-gather.9.cloned.1.call-done = bf16[2,1024,767]{1,0,2:T(2,128)(2,1)} async-done(((bf16[2,512,767]{1,0,2:T(2,128)(2,1)}), bf16[2,1024,767]{1,0,2:T(2,128)(2,1)}) %all-gather.9.cloned.1.call-update) | async-done | bytes 3141648 | tf_op jit(solution)/shard_map/all_gather | solution.py:172
  280.9 39.4 %all-gather.7.cloned.1.call-done = bf16[2,1024,768]{2,1,0:T(8,128)(2,1)} async-done(((bf16[2,512,768]{2,1,0:T(8,128)(2,1)}), bf16[2,1024,768]{2,1,0:T(8,128)(2,1)}) %all-gather.7.cloned.1.call-update) | async-done | bytes 3145744 | tf_op jit(solution)/shard_map/all_gather | solution.py:155
  320.3 13.8 %multiply_convert_fusion.2 = (bf16[2048,1536]{1,0:T(8,128)(2,1)}, f32[2048,1536]{1,0:T(8,128)}) fusion(f32[1536]{0:T(1024)S(1)} %convert_element_type.208, bf16[2048,768]{1,0:T(8,128)(2,1)} %bitcast.353, bf16[768,1536]{1,0:T(8,128)(2,1)S(1)} %copy-done), kind=kOutput, calls=%fused_computation.125 | convolution fusion | flops 4863295488 | bytes 24385536 | tf_op jit(solution)/shard_map/dot_general | solution.py:156
  334.1 15.3 %fusion.97 = (bf16[1536]{0:T(1024)(128)(2,1)}, bf16[2048,1536]{1,0:T(8,128)(2,1)S(1)}) fusion(f32[2048,1536]{1,0:T(8,128)} %get-tuple-element.273, f32[1536]{0:T(1024)S(1)} %convert_element_type.208, bf16[2048,767]{0,1:T(8,128)(2,1)S(1)} %bitcast.318, bf16[1536,767]{1,0:T(8,128)(2,1)S(1)} %copy-done.63), kind=kOutput, calls=%fused_computation.195 | convolution fusion | flops 4894751232 | bytes 24381440 | tf_op jit(solution)/shard_map/dot_general | solution.py:177
  362.0 37.4 %reduce-scatter.18.cloned.1.call-done = bf16[2,512,768]{2,1,0:T(8,128)(2,1)} async-done(((bf16[2,1024,768]{2,1,0:T(8,128)(2,1)}), bf16[2,512,768]{2,1,0:T(8,128)(2,1)}) %reduce-scatter.18.cloned.1.call-update) | async-done | bytes 1572880 | tf_op jit(solution)/shard_map/reduce_scatter | solution.py:186
  412.4 44.9 %all-gather.11.cloned.1.call-done = bf16[2,1024,767]{1,0,2:T(2,128)(2,1)} async-done(((bf16[2,512,767]{1,0,2:T(2,128)(2,1)}), bf16[2,1024,767]{1,0,2:T(2,128)(2,1)}) %all-gather.11.cloned.1.call-update) | async-done | bytes 3141648 | tf_op jit(solution)/shard_map/all_gather | solution.py:194
  472.5 133.8 %while.27 = (s32[]{:T(128)}, bf16[2,1024,6,64]{1,3,2,0:T(8,128)(2,1)}, bf16[2,1024,6,64]{1,3,2,0:T(8,128)(2,1)}, bf16[2,1024,6,64]{1,3,2,0:T(8,128)(2,1)}, bf16[...) while((s32[]{:T(128)}, ...), condition=%wide.region_17.18_spmd, body=%wide.region_14.17_spmd.sunk | while | flops 4128632320 | bytes 286275584 | solution.py:203
  501.2 9.6 multiply_convert_fusion.7
  567.8 9.6 multiply_convert_fusion.7
  638.5 9.4 convolution_convert_fusion
  648.0 9.4 convolution_convert_fusion.1
  678.5 25.3 %reduce-scatter.26.cloned.1.call-done = bf16[384,767]{1,0:T(8,128)(2,1)} async-done(((bf16[1536,767]{1,0:T(8,128)(2,1)}), bf16[384,767]{1,0:T(8,128)(2,1)}) %reduce-scatter.26.cloned.1.call-update) | async-done | bytes 589072 | tf_op jit(solution)/shard_map/reduce_scatter | solution.py:261
  703.8 35.6 %reduce-scatter.24.cloned.1.call-done = bf16[192,1536]{1,0:T(8,128)(2,1)} async-done(((bf16[768,1536]{1,0:T(8,128)(2,1)}), bf16[192,1536]{1,0:T(8,128)(2,1)}) %reduce-scatter.24.cloned.1.call-update) | async-done | bytes 589840 | tf_op jit(solution)/shard_map/reduce_scatter | solution.py:255
  739.4 25.2 %reduce-scatter.22.cloned.1.call-done = bf16[96,767]{1,0:T(8,128)(2,1)} async-done(((bf16[384,767]{1,0:T(8,128)(2,1)}), bf16[96,767]{1,0:T(8,128)(2,1)}) %reduce-scatter.22.cloned.1.call-update) | async-done | bytes 147280 | tf_op jit(solution)/shard_map/reduce_scatter | solution.py:252
  771.7 9.1 bitcast_convert_fusion
  792.0 18.4 %reduce-scatter.16.cloned.1.call-done = bf16[2,512,767]{2,1,0:T(8,128)(2,1)} async-done(((bf16[2,1024,767]{2,1,0:T(8,128)(2,1)}), bf16[2,512,767]{2,1,0:T(8,128)(2,1)}) %reduce-scatter.16.cloned.1.call-update) | async-done | bytes 1570832 | tf_op jit(solution)/shard_map/reduce_scatter | solution.py:164
  818.3 14.5 %reduce-scatter.30.cloned.1.call-done = bf16[96,2]{1,0:T(8,128)(2,1)} async-done(((bf16[384,2]{1,0:T(8,128)(2,1)}), bf16[96,2]{1,0:T(8,128)(2,1)}) %reduce-scatter.30.cloned.1.call-update) | async-done | bytes 400
  833.6 11.8 %all-reduce.2 = (bf16[2,96]{1,0:T(2,128)(2,1)S(1)}, bf16[384]{0:T(512)(128)(2,1)S(1)}) all-reduce(bf16[2,96]{1,0:T(2,128)(2,1)S(1)} %copy.97, bf16[384]{0:T(512)(128)(2,1)S(1)} %dynamic-slice.1), channel_id=1, replica_groups=mesh['dp'=4,'group'=4,'tensor'=2] {'group'}, use_global_device_ids=true, to_apply=%region_28.29 | all-reduce | flops 576 | bytes 2304 | tf_op jit(solution)/shard_map/psum | solution.py:267
  846.5 71.2 %all-reduce.6.cloned.1.call-done = (bf16[3,192,384]{1,2,0:T(8,128)(2,1)}, bf16[96,767]{1,0:T(8,128)(2,1)}, bf16[192,1536]{1,0:T(8,128)(2,1)}, bf16[384,767]{1,0:T(8,128)(2,1)}) async-done(((bf16[3,192,384]{1,2,0:T(8,128)(2,1)}, bf16[96,767]{1,0:T(8,128)(2,1)}, bf16[192,1536]{1,0:T(8,128)(2,1)}, bf16[384,767]{1,0:T(8,128)(2,1)}), (bf16[3,192,384]{1,2,0:T(8,128)(2,1)}, bf16[96,767]{1,0:T(8,128)(2,1)}, ...) | async-done | bytes 1768528 | tf_op jit(solution)/shard_map/psum | solution.py:266
  926.1 36.2 %reduce-scatter.20.cloned.1.call-done = bf16[2,512,768]{2,1,0:T(8,128)(2,1)} async-done(((bf16[2,1024,768]{2,1,0:T(8,128)(2,1)}), bf16[2,512,768]{2,1,0:T(8,128)(2,1)}) %reduce-scatter.20.cloned.1.call-update) | async-done | bytes 1572880 | tf_op jit(solution)/shard_map/reduce_scatter | solution.py:222
  979.7 39.6 %all-reduce.1 = (f32[2,768]{1,0:T(2,128)}, f32[2,767]{1,0:T(2,128)}) all-reduce(f32[2,768]{1,0:T(2,128)S(1)} %pad_maximum_fusion.4, f32[2,767]{1,0:T(2,128)S(1)} %pad_maximum_fusion.5), channel_id=1, replica_groups=mesh['dp'=4,'group'=4,'tensor'=2] {'dp','group','tensor'}, use_global_device_ids=true, to_apply=%region_22.23 | all-reduce | flops 3070 | bytes 24560 | tf_op jit(solution)/shard_map/psum | solution.py:236
  (395 shorter events, 414.3 us)
Async XLA Ops:
  7.2 313.1 %copy-start = (bf16[768,1536]{1,0:T(8,128)(2,1)S(1)}, bf16[768,1536]{1,0:T(8,128)(2,1)}, u32[]{:S(2)}) copy-start(bf16[768,1536]{1,0:T(8,128)(2,1)} %param.21) | copy-start | bytes 7077892
  7.2 69.0 %all-gather.5.cloned.1.call-start = ((), (), s32[]{:S(2)}) async-start(), calls=%async_computation.9 | async-start | bytes 4718592 | tf_op jit(solution)/shard_map/all_gather | solution.py:128
  28.4 199.0 %reduce-scatter.14.cloned.1.call-start = ((), (), s32[]{:S(2)}) async-start(), calls=%async_computation.10 | async-start | bytes 4718592 | tf_op jit(solution)/shard_map/reduce_scatter | solution.py:149
  124.6 54.4 %copy-start.65 = (bf16[384,767]{1,0:T(8,128)(2,1)S(1)}, bf16[384,767]{1,0:T(8,128)(2,1)}, u32[]{:S(2)}) copy-start(bf16[384,767]{1,0:T(8,128)(2,1)} %param.20) | copy-start | bytes 1767172
  183.9 90.0 %all-gather.9.cloned.1.call-start = ((), (), s32[]{:S(2)}) async-start(), calls=%async_computation.13 | async-start | bytes 4712448 | tf_op jit(solution)/shard_map/all_gather | solution.py:172
  184.6 135.7 %all-gather.7.cloned.1.call-start = ((), (), s32[]{:S(2)}) async-start(), calls=%async_computation.11 | async-start | bytes 4718592 | tf_op jit(solution)/shard_map/all_gather | solution.py:155
  244.4 155.0 %reduce-scatter.18.cloned.1.call-start = ((), (), s32[]{:S(2)}) async-start(), calls=%async_computation.14 | async-start | bytes 4718592 | tf_op jit(solution)/shard_map/reduce_scatter | solution.py:186
  355.9 101.4 %all-gather.11.cloned.1.call-start = ((), (), s32[]{:S(2)}) async-start(), calls=%async_computation.15 | async-start | bytes 4712448 | tf_op jit(solution)/shard_map/all_gather | solution.py:194
  359.5 39.9 %copy-start.11 = (f32[2,512,767]{2,1,0:T(8,128)S(1)}, f32[2,512,767]{2,1,0:T(8,128)}, u32[]{:S(2)}) copy-start(f32[2,512,767]{2,1,0:T(8,128)} %get-tuple-element.243) | copy-start | bytes 9424900
  412.3 263.4 %reduce-scatter.28.cloned.1.call-start = ((), (), s32[]{:S(2)}) async-start(), calls=%async_computation.20 | async-start | bytes 2211840
  638.5 65.3 %reduce-scatter.26.cloned.1.call-start = ((), (), s32[]{:S(2)}) async-start(), calls=%async_computation.19 | async-start | bytes 2949120 | tf_op jit(solution)/shard_map/reduce_scatter | solution.py:261
  647.9 91.5 %reduce-scatter.24.cloned.1.call-start = ((), (), s32[]{:S(2)}) async-start(), calls=%async_computation.18 | async-start | bytes 2949120 | tf_op jit(solution)/shard_map/reduce_scatter | solution.py:255
  657.4 107.2 %reduce-scatter.22.cloned.1.call-start = ((), (), s32[]{:S(2)}) async-start(), calls=%async_computation.17 | async-start | bytes 737280 | tf_op jit(solution)/shard_map/reduce_scatter | solution.py:252
  663.4 146.9 %reduce-scatter.16.cloned.1.call-start = ((), (), s32[]{:S(2)}) async-start(), calls=%async_computation.12 | async-start | bytes 4718592 | tf_op jit(solution)/shard_map/reduce_scatter | solution.py:164
  672.5 160.2 %reduce-scatter.30.cloned.1.call-start = ((), (), s32[]{:S(2)}) async-start(), calls=%async_computation.21 | async-start | bytes 122880
  675.7 242.0 %all-reduce.6.cloned.1.call-start = ((), (), s32[]{:S(2)}) async-start(), calls=%async_computation.22 | async-start | bytes 3833856 | tf_op jit(solution)/shard_map/psum | solution.py:266
  764.6 197.6 %reduce-scatter.20.cloned.1.call-start = ((), (), s32[]{:S(2)}) async-start(), calls=%async_computation.16 | async-start | bytes 4718592 | tf_op jit(solution)/shard_map/reduce_scatter | solution.py:222
  780.8 29.5 %copy-start.12 = (f32[2,512,767]{2,1,0:T(8,128)S(1)}, f32[2,512,767]{2,1,0:T(8,128)}, u32[]{:S(2)}) copy-start(f32[2,512,767]{2,1,0:T(8,128)} %get-tuple-element.243) | copy-start | bytes 9424900
  780.8 29.5 %copy-start.55 = (f32[767]{0:T(1024)S(1)}, f32[767]{0:T(1024)}, u32[]{:S(2)}) copy-start(f32[767]{0:T(1024)} %get-tuple-element.192) | copy-start | bytes 9208
  818.2 144.0 %copy-start.10 = (f32[2,512,767]{2,1,0:T(8,128)S(1)}, f32[2,512,767]{2,1,0:T(8,128)}, u32[]{:S(2)}) copy-start(f32[2,512,767]{2,1,0:T(8,128)} %convert_element_type.195) | copy-start | bytes 9424900
  818.2 144.0 %copy-start.41 = (f32[768]{0:T(1024)S(1)}, f32[768]{0:T(1024)}, u32[]{:S(2)}) copy-start(f32[768]{0:T(1024)} %copy-done.40) | copy-start | bytes 9220
  818.2 144.0 %copy-start.46 = (f32[2,512]{1,0:T(2,128)S(1)}, f32[2,512]{1,0:T(2,128)}, u32[]{:S(2)}) copy-start(f32[2,512]{1,0:T(2,128)} %copy-done.45) | copy-start | bytes 12292
  923.8 41.2 %copy-start.50 = (f32[1024]{0:T(1024)S(1)}, f32[1024]{0:T(1024)}, u32[]{:S(2)}) copy-start(f32[1024]{0:T(1024)} %copy-done.49) | copy-start | bytes 12292
  972.1 47.2 %copy-start.1 = (bf16[768,1536]{1,0:T(8,128)(2,1)S(1)}, bf16[768,1536]{1,0:T(8,128)(2,1)}, u32[]{:S(2)}) copy-start(bf16[768,1536]{1,0:T(8,128)(2,1)} %param.21) | copy-start | bytes 7077892
  (77 other events, 307.3 us)
Sparse Core Ops, SparseCore 0:
  28.5 47.6 all-gather.4
  184.0 43.3 reduce-scatter.13
  229.0 44.8 all-gather.8
  275.3 44.9 all-gather.6
  356.0 43.3 reduce-scatter.17
  412.4 44.8 all-gather.10
  638.6 29.3 reduce-scatter.27
  670.7 33.0 reduce-scatter.25
  706.3 33.0 reduce-scatter.23
  742.5 22.0 reduce-scatter.21
  766.9 43.3 reduce-scatter.15
  813.2 19.5 reduce-scatter.29
  836.0 81.7 all-reduce.5
  919.8 42.3 reduce-scatter.19
where the time goes:
time: 1040 us; the launch traced here: 1030 us
  waiting for transfers between devices  468 us (45%)
  matrix products  207 us (20%)
  local copies, waits for them, and re-layouts  161 us (15%)
  other arithmetic  114 us (11%)
  blocking collectives  57.5 us (6%)
  between operations  15.8 us (2%)
    psum x1, waiting for transfers between devices, on_device(): lax.psum(shards[0].astype(jnp.bfloat16), 'group').astype(jnp.float32)  71.2 us
    unnamed x134, local copies, waits for them, and re-layouts  50.8 us
    all_gather x1, waiting for transfers between devices, on_device(): full_one = lax.all_gather(one_low, 'tensor', axis=1, tiled=True)  47.5 us
    all_gather x1, waiting for transfers between devices, on_device(): lax.all_gather(branch_seq, 'tensor', axis=1, tiled=True)  44.9 us
    reduce_scatter x1, waiting for transfers between devices, on_device(): lax.psum_scatter(branch_part.astype(jnp.bfloat16), 'tensor', scatter_dime...  42.1 us
    psum x1, blocking collectives, on_device(): lax.psum((gain_terms, bias_terms), ('dp', 'group', 'tensor'))  39.6 us
    all_gather x1, waiting for transfers between devices, on_device(): lax.all_gather(two_low, 'tensor', axis=1, tiled=True)  39.4 us
    reduce_scatter x1, waiting for transfers between devices, on_device(): lax.psum_scatter(two_part.astype(jnp.bfloat16), 'tensor', scatter_dimensi...  37.4 us
  transfers between devices with their start and end apart: 14, of which 13 were waited for; matrix products, arithmetic and copies ran while one was open for 10% of the time, Pallas kernels for 0%

commit v1 on v0

--- a/solution.py
+++ b/solution.py
@@ -233,7 +233,9 @@
     bias_terms = jnp.stack(
         [jnp.sum(branch_low.astype(jnp.float32), axis=0), jnp.sum(upstream_flat, axis=0)]
     )
-    grad_gains, grad_out_biases = lax.psum((gain_terms, bias_terms), ("dp", "group", "tensor"))
+    grad_gains, grad_out_biases = lax.psum(
+        lax.psum((gain_terms, bias_terms), ("group", "tensor")), "dp"
+    )
     weight_grads = (
         grad_qkv,
         grad_qv_bias,

time: 1040 us -> 1050 us (level)
    psum x1 -> x2, blocking collectives: 39.6 us -> 46.9 us  [the longest x1 36.1 us: on_device(): lax.psum((gain_terms, bias_terms), ('group', 'tensor'))]
where the time goes in v1:
time: 1050 us; the launch traced here: 1030 us
  waiting for transfers between devices  468 us (45%)
  matrix products  208 us (20%)
  local copies, waits for them, and re-layouts  161 us (15%)
  other arithmetic  114 us (11%)
  blocking collectives  64.8 us (6%)
  between operations  15.8 us (2%)
    psum x1, waiting for transfers between devices, on_device(): lax.psum(shards[0].astype(jnp.bfloat16), 'group').astype(jnp.float32)  71.2 us
    unnamed x134, local copies, waits for them, and re-layouts  50.8 us
    all_gather x1, waiting for transfers between devices, on_device(): full_one = lax.all_gather(one_low, 'tensor', axis=1, tiled=True)  47.5 us
    all_gather x1, waiting for transfers between devices, on_device(): lax.all_gather(branch_seq, 'tensor', axis=1, tiled=True)  44.9 us
    reduce_scatter x1, waiting for transfers between devices, on_device(): lax.psum_scatter(branch_part.astype(jnp.bfloat16), 'tensor', scatter_dime...  42.1 us
    all_gather x1, waiting for transfers between devices, on_device(): lax.all_gather(two_low, 'tensor', axis=1, tiled=True)  39.4 us
    reduce_scatter x1, waiting for transfers between devices, on_device(): lax.psum_scatter(two_part.astype(jnp.bfloat16), 'tensor', scatter_dimensi...  37.4 us
    reduce_scatter x1, waiting for transfers between devices, on_device(): lax.psum_scatter(one_part.astype(jnp.bfloat16), 'tensor', scatter_dimensi...  36.2 us
  transfers between devices with their start and end apart: 14, of which 13 were waited for; matrix products, arithmetic and copies ran while one was open for 10% of the time, Pallas kernels for 0%

profile of v1, /device:TPU:0, one launch (start us, length us, event | category | flops | bytes accessed | tf_op | source)
XLA Modules:
  0.0 1033.7 jit_solution(865305445205281709)
XLA Ops:
  28.7 47.5 %all-gather.5.cloned.1.call-done = bf16[2,1024,768]{2,1,0:T(8,128)(2,1)} async-done(((bf16[2,512,768]{2,1,0:T(8,128)(2,1)}), bf16[2,1024,768]{2,1,0:T(8,128)(2,1)}) %all-gather.5.cloned.1.call-update) | async-done | bytes 3145744 | tf_op jit(solution)/shard_map/all_gather | solution.py:128
  124.7 54.3 %while.26 = (s32[]{:T(128)}, bf16[2,1024,6,64]{1,3,2,0:T(8,128)(2,1)}, f32[2,6,1024]{2,1,0:T(8,128)}, bf16[2,1024,6,64]{1,3,2,0:T(8,128)(2,1)}, s32[2,1024]{1,0:...) while((s32[]{:T(128)}, ...), condition=%wide.region_7.8_spmd, body=%wide.region_2.7_spmd.sunk | while | flops 1692272128 | bytes 111457016 | solution.py:144
  185.3 42.1 %reduce-scatter.14.cloned.1.call-done = bf16[2,512,767]{2,1,0:T(8,128)(2,1)} async-done(((bf16[2,1024,767]{2,1,0:T(8,128)(2,1)}), bf16[2,512,767]{2,1,0:T(8,128)(2,1)}) %reduce-scatter.14.cloned.1.call-update) | async-done | bytes 1570832 | tf_op jit(solution)/shard_map/reduce_scatter | solution.py:149
  244.5 29.4 %all-gather.9.cloned.1.call-done = bf16[2,1024,767]{1,0,2:T(2,128)(2,1)} async-done(((bf16[2,512,767]{1,0,2:T(2,128)(2,1)}), bf16[2,1024,767]{1,0,2:T(2,128)(2,1)}) %all-gather.9.cloned.1.call-update) | async-done | bytes 3141648 | tf_op jit(solution)/shard_map/all_gather | solution.py:172
  280.9 39.4 %all-gather.7.cloned.1.call-done = bf16[2,1024,768]{2,1,0:T(8,128)(2,1)} async-done(((bf16[2,512,768]{2,1,0:T(8,128)(2,1)}), bf16[2,1024,768]{2,1,0:T(8,128)(2,1)}) %all-gather.7.cloned.1.call-update) | async-done | bytes 3145744 | tf_op jit(solution)/shard_map/all_gather | solution.py:155
  320.4 13.9 %multiply_convert_fusion.2 = (bf16[2048,1536]{1,0:T(8,128)(2,1)}, f32[2048,1536]{1,0:T(8,128)}) fusion(f32[1536]{0:T(1024)S(1)} %convert_element_type.208, bf16[2048,768]{1,0:T(8,128)(2,1)} %bitcast.353, bf16[768,1536]{1,0:T(8,128)(2,1)S(1)} %copy-done), kind=kOutput, calls=%fused_computation.125 | convolution fusion | flops 4863295488 | bytes 24385536 | tf_op jit(solution)/shard_map/dot_general | solution.py:156
  334.3 15.3 %fusion.97 = (bf16[1536]{0:T(1024)(128)(2,1)}, bf16[2048,1536]{1,0:T(8,128)(2,1)S(1)}) fusion(f32[2048,1536]{1,0:T(8,128)} %get-tuple-element.275, f32[1536]{0:T(1024)S(1)} %convert_element_type.208, bf16[2048,767]{0,1:T(8,128)(2,1)S(1)} %bitcast.318, bf16[1536,767]{1,0:T(8,128)(2,1)S(1)} %copy-done.63), kind=kOutput, calls=%fused_computation.195 | convolution fusion | flops 4894751232 | bytes 24381440 | tf_op jit(solution)/shard_map/dot_general | solution.py:177
  362.1 37.4 %reduce-scatter.18.cloned.1.call-done = bf16[2,512,768]{2,1,0:T(8,128)(2,1)} async-done(((bf16[2,1024,768]{2,1,0:T(8,128)(2,1)}), bf16[2,512,768]{2,1,0:T(8,128)(2,1)}) %reduce-scatter.18.cloned.1.call-update) | async-done | bytes 1572880 | tf_op jit(solution)/shard_map/reduce_scatter | solution.py:186
  412.6 44.9 %all-gather.11.cloned.1.call-done = bf16[2,1024,767]{1,0,2:T(2,128)(2,1)} async-done(((bf16[2,512,767]{1,0,2:T(2,128)(2,1)}), bf16[2,1024,767]{1,0,2:T(2,128)(2,1)}) %all-gather.11.cloned.1.call-update) | async-done | bytes 3141648 | tf_op jit(solution)/shard_map/all_gather | solution.py:194
  472.6 133.9 %while.27 = (s32[]{:T(128)}, bf16[2,1024,6,64]{1,3,2,0:T(8,128)(2,1)}, bf16[2,1024,6,64]{1,3,2,0:T(8,128)(2,1)}, bf16[2,1024,6,64]{1,3,2,0:T(8,128)(2,1)}, bf16[...) while((s32[]{:T(128)}, ...), condition=%wide.region_17.18_spmd, body=%wide.region_14.17_spmd.sunk | while | flops 4128632320 | bytes 286275584 | solution.py:203
  501.4 9.6 multiply_convert_fusion.7
  568.0 9.6 multiply_convert_fusion.7
  638.7 9.3 convolution_convert_fusion
  648.2 9.4 convolution_convert_fusion.1
  678.7 25.3 %reduce-scatter.26.cloned.1.call-done = bf16[384,767]{1,0:T(8,128)(2,1)} async-done(((bf16[1536,767]{1,0:T(8,128)(2,1)}), bf16[384,767]{1,0:T(8,128)(2,1)}) %reduce-scatter.26.cloned.1.call-update) | async-done | bytes 589072 | tf_op jit(solution)/shard_map/reduce_scatter | solution.py:263
  704.0 35.6 %reduce-scatter.24.cloned.1.call-done = bf16[192,1536]{1,0:T(8,128)(2,1)} async-done(((bf16[768,1536]{1,0:T(8,128)(2,1)}), bf16[192,1536]{1,0:T(8,128)(2,1)}) %reduce-scatter.24.cloned.1.call-update) | async-done | bytes 589840 | tf_op jit(solution)/shard_map/reduce_scatter | solution.py:257
  739.6 25.2 %reduce-scatter.22.cloned.1.call-done = bf16[96,767]{1,0:T(8,128)(2,1)} async-done(((bf16[384,767]{1,0:T(8,128)(2,1)}), bf16[96,767]{1,0:T(8,128)(2,1)}) %reduce-scatter.22.cloned.1.call-update) | async-done | bytes 147280 | tf_op jit(solution)/shard_map/reduce_scatter | solution.py:254
  792.2 18.3 %reduce-scatter.16.cloned.1.call-done = bf16[2,512,767]{2,1,0:T(8,128)(2,1)} async-done(((bf16[2,1024,767]{2,1,0:T(8,128)(2,1)}), bf16[2,512,767]{2,1,0:T(8,128)(2,1)}) %reduce-scatter.16.cloned.1.call-update) | async-done | bytes 1570832 | tf_op jit(solution)/shard_map/reduce_scatter | solution.py:164
  818.5 14.5 %reduce-scatter.30.cloned.1.call-done = bf16[96,2]{1,0:T(8,128)(2,1)} async-done(((bf16[384,2]{1,0:T(8,128)(2,1)}), bf16[96,2]{1,0:T(8,128)(2,1)}) %reduce-scatter.30.cloned.1.call-update) | async-done | bytes 400
  833.7 11.8 %all-reduce.3 = (bf16[2,96]{1,0:T(2,128)(2,1)S(1)}, bf16[384]{0:T(512)(128)(2,1)S(1)}) all-reduce(bf16[2,96]{1,0:T(2,128)(2,1)S(1)} %copy.97, bf16[384]{0:T(512)(128)(2,1)S(1)} %dynamic-slice.1), channel_id=1, replica_groups=mesh['dp'=4,'group'=4,'tensor'=2] {'group'}, use_global_device_ids=true, to_apply=%region_29.30 | all-reduce | flops 576 | bytes 2304 | tf_op jit(solution)/shard_map/psum | solution.py:269
  846.7 71.2 %all-reduce.7.cloned.1.call-done = (bf16[3,192,384]{1,2,0:T(8,128)(2,1)}, bf16[96,767]{1,0:T(8,128)(2,1)}, bf16[192,1536]{1,0:T(8,128)(2,1)}, bf16[384,767]{1,0:T(8,128)(2,1)}) async-done(((bf16[3,192,384]{1,2,0:T(8,128)(2,1)}, bf16[96,767]{1,0:T(8,128)(2,1)}, bf16[192,1536]{1,0:T(8,128)(2,1)}, bf16[384,767]{1,0:T(8,128)(2,1)}), (bf16[3,192,384]{1,2,0:T(8,128)(2,1)}, bf16[96,767]{1,0:T(8,128)(2,1)}, ...) | async-done | bytes 1768528 | tf_op jit(solution)/shard_map/psum | solution.py:268
  926.2 36.2 %reduce-scatter.20.cloned.1.call-done = bf16[2,512,768]{2,1,0:T(8,128)(2,1)} async-done(((bf16[2,1024,768]{2,1,0:T(8,128)(2,1)}), bf16[2,512,768]{2,1,0:T(8,128)(2,1)}) %reduce-scatter.20.cloned.1.call-update) | async-done | bytes 1572880 | tf_op jit(solution)/shard_map/reduce_scatter | solution.py:222
  979.9 36.1 %all-reduce.1 = (f32[2,768]{1,0:T(2,128)S(1)}, f32[2,767]{1,0:T(2,128)S(1)}) all-reduce(f32[2,768]{1,0:T(2,128)S(1)} %pad_maximum_fusion.4, f32[2,767]{1,0:T(2,128)S(1)} %pad_maximum_fusion.5), channel_id=1, replica_groups=mesh['dp'=4,'group'=4,'tensor'=2] {'group','tensor'}, use_global_device_ids=true, to_apply=%region_22.23 | all-reduce | flops 3070 | bytes 24560 | tf_op jit(solution)/shard_map/psum | solution.py:237
  1016.0 10.7 %all-reduce.2 = (f32[2,768]{1,0:T(2,128)}, f32[2,767]{1,0:T(2,128)}) all-reduce(f32[2,768]{1,0:T(2,128)S(1)} %get-tuple-element.232, f32[2,767]{1,0:T(2,128)S(1)} %get-tuple-element.233), channel_id=1, replica_groups=mesh['dp'=4,'group'=4,'tensor'=2] {'dp'}, use_global_device_ids=true, to_apply=%region_23.24 | all-reduce | flops 3070 | bytes 24560 | tf_op jit(solution)/shard_map/psum | solution.py:236
  (396 shorter events, 423.7 us)
Async XLA Ops:
  7.2 313.2 %copy-start = (bf16[768,1536]{1,0:T(8,128)(2,1)S(1)}, bf16[768,1536]{1,0:T(8,128)(2,1)}, u32[]{:S(2)}) copy-start(bf16[768,1536]{1,0:T(8,128)(2,1)} %param.21) | copy-start | bytes 7077892
  7.2 69.0 %all-gather.5.cloned.1.call-start = ((), (), s32[]{:S(2)}) async-start(), calls=%async_computation.9 | async-start | bytes 4718592 | tf_op jit(solution)/shard_map/all_gather | solution.py:128
  28.4 199.0 %reduce-scatter.14.cloned.1.call-start = ((), (), s32[]{:S(2)}) async-start(), calls=%async_computation.10 | async-start | bytes 4718592 | tf_op jit(solution)/shard_map/reduce_scatter | solution.py:149
  124.7 54.4 %copy-start.65 = (bf16[384,767]{1,0:T(8,128)(2,1)S(1)}, bf16[384,767]{1,0:T(8,128)(2,1)}, u32[]{:S(2)}) copy-start(bf16[384,767]{1,0:T(8,128)(2,1)} %param.20) | copy-start | bytes 1767172
  183.9 90.0 %all-gather.9.cloned.1.call-start = ((), (), s32[]{:S(2)}) async-start(), calls=%async_computation.13 | async-start | bytes 4712448 | tf_op jit(solution)/shard_map/all_gather | solution.py:172
  184.7 135.7 %all-gather.7.cloned.1.call-start = ((), (), s32[]{:S(2)}) async-start(), calls=%async_computation.11 | async-start | bytes 4718592 | tf_op jit(solution)/shard_map/all_gather | solution.py:155
  244.5 155.1 %reduce-scatter.18.cloned.1.call-start = ((), (), s32[]{:S(2)}) async-start(), calls=%async_computation.14 | async-start | bytes 4718592 | tf_op jit(solution)/shard_map/reduce_scatter | solution.py:186
  356.0 101.5 %all-gather.11.cloned.1.call-start = ((), (), s32[]{:S(2)}) async-start(), calls=%async_computation.15 | async-start | bytes 4712448 | tf_op jit(solution)/shard_map/all_gather | solution.py:194
  359.6 39.9 %copy-start.11 = (f32[2,512,767]{2,1,0:T(8,128)S(1)}, f32[2,512,767]{2,1,0:T(8,128)}, u32[]{:S(2)}) copy-start(f32[2,512,767]{2,1,0:T(8,128)} %get-tuple-element.245) | copy-start | bytes 9424900
  412.5 263.4 %reduce-scatter.28.cloned.1.call-start = ((), (), s32[]{:S(2)}) async-start(), calls=%async_computation.20 | async-start | bytes 2211840
  638.7 65.3 %reduce-scatter.26.cloned.1.call-start = ((), (), s32[]{:S(2)}) async-start(), calls=%async_computation.19 | async-start | bytes 2949120 | tf_op jit(solution)/shard_map/reduce_scatter | solution.py:263
  648.1 91.5 %reduce-scatter.24.cloned.1.call-start = ((), (), s32[]{:S(2)}) async-start(), calls=%async_computation.18 | async-start | bytes 2949120 | tf_op jit(solution)/shard_map/reduce_scatter | solution.py:257
  657.5 107.2 %reduce-scatter.22.cloned.1.call-start = ((), (), s32[]{:S(2)}) async-start(), calls=%async_computation.17 | async-start | bytes 737280 | tf_op jit(solution)/shard_map/reduce_scatter | solution.py:254
  663.6 147.0 %reduce-scatter.16.cloned.1.call-start = ((), (), s32[]{:S(2)}) async-start(), calls=%async_computation.12 | async-start | bytes 4718592 | tf_op jit(solution)/shard_map/reduce_scatter | solution.py:164
  672.7 160.3 %reduce-scatter.30.cloned.1.call-start = ((), (), s32[]{:S(2)}) async-start(), calls=%async_computation.21 | async-start | bytes 122880
  675.8 242.1 %all-reduce.7.cloned.1.call-start = ((), (), s32[]{:S(2)}) async-start(), calls=%async_computation.22 | async-start | bytes 3833856 | tf_op jit(solution)/shard_map/psum | solution.py:268
  764.8 197.6 %reduce-scatter.20.cloned.1.call-start = ((), (), s32[]{:S(2)}) async-start(), calls=%async_computation.16 | async-start | bytes 4718592 | tf_op jit(solution)/shard_map/reduce_scatter | solution.py:222
  781.1 29.5 %copy-start.12 = (f32[2,512,767]{2,1,0:T(8,128)S(1)}, f32[2,512,767]{2,1,0:T(8,128)}, u32[]{:S(2)}) copy-start(f32[2,512,767]{2,1,0:T(8,128)} %get-tuple-element.245) | copy-start | bytes 9424900
  781.1 29.5 %copy-start.55 = (f32[767]{0:T(1024)S(1)}, f32[767]{0:T(1024)}, u32[]{:S(2)}) copy-start(f32[767]{0:T(1024)} %get-tuple-element.192) | copy-start | bytes 9208
  818.4 144.0 %copy-start.10 = (f32[2,512,767]{2,1,0:T(8,128)S(1)}, f32[2,512,767]{2,1,0:T(8,128)}, u32[]{:S(2)}) copy-start(f32[2,512,767]{2,1,0:T(8,128)} %convert_element_type.195) | copy-start | bytes 9424900
  818.4 144.0 %copy-start.41 = (f32[768]{0:T(1024)S(1)}, f32[768]{0:T(1024)}, u32[]{:S(2)}) copy-start(f32[768]{0:T(1024)} %copy-done.40) | copy-start | bytes 9220
  818.4 144.0 %copy-start.46 = (f32[2,512]{1,0:T(2,128)S(1)}, f32[2,512]{1,0:T(2,128)}, u32[]{:S(2)}) copy-start(f32[2,512]{1,0:T(2,128)} %copy-done.45) | copy-start | bytes 12292
  924.0 41.2 %copy-start.50 = (f32[1024]{0:T(1024)S(1)}, f32[1024]{0:T(1024)}, u32[]{:S(2)}) copy-start(f32[1024]{0:T(1024)} %copy-done.49) | copy-start | bytes 12292
  972.2 54.5 %copy-start.1 = (bf16[768,1536]{1,0:T(8,128)(2,1)S(1)}, bf16[768,1536]{1,0:T(8,128)(2,1)}, u32[]{:S(2)}) copy-start(bf16[768,1536]{1,0:T(8,128)(2,1)} %param.21) | copy-start | bytes 7077892
  (77 other events, 307.5 us)
Sparse Core Ops, SparseCore 0:
  28.5 47.6 all-gather.4
  184.0 43.3 reduce-scatter.13
  229.0 44.8 all-gather.8
  275.4 44.9 all-gather.6
  356.2 43.3 reduce-scatter.17
  412.6 44.8 all-gather.10
  638.8 29.3 reduce-scatter.27
  670.9 33.0 reduce-scatter.25
  706.5 33.0 reduce-scatter.23
  742.7 22.0 reduce-scatter.21
  767.1 43.3 reduce-scatter.15
  813.4 19.5 reduce-scatter.29
  836.2 81.6 all-reduce.6
  920.0 42.3 reduce-scatter.19
